TPU v7x, 256 devices: a whole 4x4x8 slice. The times are simulated.
256 devices in a mesh: ctx: 32 (over x, z), grp: 8 (over y, core).
Axes of the slice: x: 4, y: 4, z: 8, core: 2. Of those that a mesh axis runs over, the one named last changes fastest.
Arguments:
- out_grad: bfloat16 [16384, 2048], P('ctx', 'grp'), may hold values from -6 to 6
- filter_mats: bfloat16 [16, 2048, 2048], P('grp', 'ctx'), may hold values from -0.125 to 0.125
- coeffs: float32 [16, 80], replicated, may hold values from -0.15625 to 0.15625
- pole_rates: float32 [80], replicated, may hold values from 1.2207031e-06 to 0.03
Outputs:
- in_grad: bfloat16 [16384, 2048], P('ctx', 'grp')
All inputs are finite; a program needn't handle non-finite values.
Results may differ from a plain program's by a relative error of at most 0.001.
Values may be sent and summed in bfloat16 or wider, within the bound.
A program may use at most 128 MiB of HBM per device.

v0:
```python
import jax
import jax.numpy as jnp
from jax import lax
from jax.sharding import PartitionSpec as P

exact_prec = lax.Precision.HIGHEST


def entering(array, axis, combine, identity):
    count, here = (lax.axis_size(axis), lax.axis_index(axis))
    everything = jax.tree.map(lambda part: lax.all_gather(part, axis), array)
    start = jax.tree.map(
        lambda part, zero: jnp.broadcast_to(jnp.asarray(zero, part.dtype), part.shape),
        array,
        identity,
    )

    def step(k, before):
        at = count - 1 - k
        reached = at > here
        new = combine(before, jax.tree.map(lambda part: part[at], everything))
        return jax.tree.map(lambda a, b: jnp.where(reached, a, b), new, before)

    return lax.fori_loop(0, count, step, start)


def merge_suffix(earlier, latter):
    carried_e, factor_e = earlier
    carried_l, factor_l = latter
    return (carried_l + factor_l * carried_e, factor_l * factor_e)


def per_device(out_grad, filter_mats, coeffs, pole_rates):
    full_grad = lax.all_gather(out_grad, "grp", axis=1, tiled=True)
    length = full_grad.shape[0]
    col_width = out_grad.shape[1]
    poles = pole_rates.shape[0]
    positions = jnp.arange(length, dtype=jnp.float32)
    pole_gains = jnp.sqrt(-jnp.expm1(-2.0 * pole_rates))
    middle = float(length // 2)
    rising = jnp.exp(-(positions[:, None] - middle) * pole_rates[None, :])
    falling = jnp.exp((positions[:, None] - middle) * pole_rates[None, :])
    causal = positions[:, None] >= positions[None, :]
    decay_pos = jnp.exp(-positions[:, None] * pole_rates[None, :])
    edge_decay = pole_gains[None, :] * jnp.exp(-(length - positions)[:, None] * pole_rates[None, :])
    block_decay = jnp.exp(-length * pole_rates)[:, None]
    unit_factor = jnp.ones((poles, 1), jnp.float32)
    filters = filter_mats.shape[0]
    own_coeffs = lax.dynamic_slice_in_dim(coeffs, lax.axis_index("grp") * filters, filters, 0)
    kernel_mat = jnp.einsum(
        "tp,kp,sp->kts", rising, own_coeffs * pole_gains[None, :], falling, precision=exact_prec
    )
    kernel_mat = jnp.where(causal[None], kernel_mat, 0.0)
    weights = own_coeffs[:, :, None] * decay_pos.T[None]
    proj_grad = jnp.einsum(
        "tj,kij->kti",
        full_grad,
        lax.all_gather(filter_mats, "ctx", axis=1, tiled=True),
        preferred_element_type=jnp.float32,
    )
    near_part = jnp.einsum("kts,kti->si", kernel_mat, proj_grad, precision=exact_prec)
    pole_part = jnp.einsum("kpt,kti->pi", weights, proj_grad, precision=exact_prec)
    stacked = jnp.concatenate([near_part, pole_part], axis=0)
    near_sum = lax.psum_scatter(stacked[:length], "grp", scatter_dimension=1, tiled=True)
    pole_sum = lax.psum(stacked[length:], "grp")
    later_all = entering(
        (pole_sum, block_decay), "ctx", merge_suffix, (jnp.zeros_like(pole_sum), unit_factor)
    )[0]
    own_cols = lax.dynamic_slice_in_dim(later_all, lax.axis_index("grp") * col_width, col_width, 1)
    total = near_sum + jnp.dot(edge_decay, own_cols, precision=exact_prec)
    return total.astype(jnp.bfloat16)


def solution(mesh):
    placed = (P("ctx", "grp"), P("grp", "ctx", None), P(), P())
    return jax.shard_map(
        per_device, mesh=mesh, in_specs=placed, out_specs=P("ctx", "grp"), check_vma=False
    )
```

profile of v0, /device:TPU:1, one launch (start us, length us, event | category | flops | bytes accessed | tf_op | source)
XLA Modules:
  0.0 488.3 jit_solution(5679977234924721466)
XLA Ops:
  8.1 1.3 dynamic-slice
  12.2 30.6 %all-gather.7.cloned.1.call-done = bf16[512,2048]{1,0:T(8,128)(2,1)} async-done(((bf16[512,256]{1,0:T(8,128)(2,1)}), bf16[512,2048]{1,0:T(8,128)(2,1)}) %all-gather.7.cloned.1.call-update) | async-done | bytes 2097168 | tf_op jit(solution)/shard_map/all_gather | solution.py:34
  42.9 141.9 %all-gather.5.cloned.1.call-done = bf16[2,2048,2048]{2,1,0:T(8,128)(2,1)} async-done(((bf16[2,64,2048]{2,1,0:T(8,128)(2,1)}), bf16[2,2048,2048]{2,1,0:T(8,128)(2,1)}) %all-gather.5.cloned.1.call-update) | async-done | bytes 16777232 | tf_op jit(solution)/shard_map/all_gather | solution.py:58
  184.8 12.9 %fusion.11 = f32[2,2048,512]{2,1,0:T(8,128)S(1)} fusion(bf16[2,2048,2048]{2,1,0:T(8,128)(2,1)} %all-gather.5.cloned.1.call-done, bf16[512,2048]{1,0:T(8,128)(2,1)} %all-gather.7.cloned.1.call-done), kind=kOutput, calls=%fused_computation.9 | convolution fusion | flops 8589934592 | bytes 27262976 | tf_op jit(solution)/shard_map/tj,kij->kti/dot_general | solution.py:55
  197.7 3.3 copy-done
  201.0 9.1 %fusion.8 = f32[1,80,2048]{2,1,0:T(8,128)} fusion(f32[2,2048,512]{2,1,0:T(8,128)S(1)} %fusion.11, f32[80,512]{1,0:T(8,128)S(1)} %multiply_exponential_fusion, f32[2,80]{1,0:T(2,128)S(1)} %get-tuple-element.167), kind=kOutput, calls=%fused_computation.8 | convolution fusion | flops 2013347840 | bytes 9208448 | tf_op jit(solution)/shard_map/kpt,kti->pi/dot_general | solution.py:62
  210.1 62.5 %all-reduce.3.cloned.1.call-done = f32[1,80,2048]{2,1,0:T(8,128)} async-done(((f32[1,80,2048]{2,1,0:T(8,128)}), f32[1,80,2048]{2,1,0:T(8,128)}) %all-reduce.3.cloned.1.call-update) | async-done | bytes 655376 | tf_op jit(solution)/shard_map/psum | solution.py:65
  272.8 119.8 %all-reduce = f32[2560]{0:T(1024)S(1)} all-reduce(f32[2560]{0:T(1024)S(1)} %get-tuple-element.168), channel_id=2, replica_groups=mesh['ctx'=32,'grp'=8] {'ctx'}, use_global_device_ids=true, to_apply=%add | all-reduce | flops 2560 | bytes 20480
  393.3 1.9 fusion.17
  395.2 17.5 %fusion.5 = f32[512,2048]{1,0:T(8,128)} fusion(f32[2,2048,512]{2,1,0:T(8,128)} %copy-done, f32[2,512,512]{1,2,0:T(8,128)S(1)} %fusion.17, pred[512,512]{0,1:T(8,128)(4,1)S(1)} %iota_compare_fusion), kind=kOutput, calls=%fused_computation.7 | convolution fusion | flops 12885426176 | bytes 14942208 | tf_op jit(solution)/shard_map/kts,kti->si/dot_general | solution.py:61
  412.7 25.1 %all-gather.9.cloned.1.call-done = f32[32,80,2048]{2,1,0:T(8,128)} async-done(((f32[1,80,2048]{2,1,0:T(8,128)}), f32[32,80,2048]{2,1,0:T(8,128)}) %all-gather.9.cloned.1.call-update) | async-done | bytes 20971536 | tf_op jit(solution)/shard_map/all_gather | solution.py:11
  437.8 41.4 %while.16 = (s32[]{:T(128)}, f32[80,2048]{1,0:T(8,128)S(1)}, s32[]{:T(128)}, f32[32,80,2048]{2,1,0:T(8,128)}, f32[32,80,1]{1,2,0:T(1,128)S(1)}, /*index=5*/s32[]{:T(128)}, s32[]{:T(128)}, s32[]{:T(128)}, s32[]{:T(128)}) while((s32[]{:T(128)}, f32[80,2048]{1,0:T(8,128)S(1)}, s32[]{:T(128)}, f32[32,80,2048]{2,1,0:T(8,128)}, ...), condition=%wide.region_3.4_spmd.clone, body=%wide.region_2.3_spmd.clone.sunk | while | flops 655368 | bytes 1967215 | solution.py:24
  448.1 1.4 fusion.39
  449.5 1.2 fusion.39
  452.1 1.2 fusion.39
  453.4 1.2 fusion.39
  454.7 1.2 fusion.39
  456.0 1.2 fusion.39
  457.3 1.3 fusion.39
  458.6 1.2 fusion.39
  459.9 1.2 fusion.39
  461.2 1.2 fusion.39
  462.5 1.2 fusion.39
  463.8 1.2 fusion.39
  465.1 1.2 fusion.39
  466.4 1.2 fusion.39
  467.7 1.2 fusion.39
  470.3 1.3 fusion.39
  471.6 1.2 fusion.39
  472.9 1.2 fusion.39
  474.1 1.2 fusion.39
  479.3 2.5 fusion.14
  (73 shorter events, 20.9 us)
Async XLA Ops:
  6.5 36.3 %all-gather.7.cloned.1.call-start = ((), (), s32[]{:S(2)}) async-start(), calls=%async_computation.2 | async-start | bytes 2359296 | tf_op jit(solution)/shard_map/all_gather | solution.py:34
  7.3 177.6 %all-gather.5.cloned.1.call-start = ((), (), s32[]{:S(2)}) async-start(), calls=%async_computation.1 | async-start | bytes 17301504 | tf_op jit(solution)/shard_map/all_gather | solution.py:58
  8.0 264.6 %all-reduce.3.cloned.1.call-start = ((), (), s32[]{:S(2)}) async-start(), calls=%async_computation.4 | async-start | bytes 1310720 | tf_op jit(solution)/shard_map/psum | solution.py:65
  197.7 3.3 copy-start
  197.7 195.3 %copy-start.1 = (f32[80]{0:T(128)S(1)}, f32[80]{0:T(128)}, u32[]{:S(2)}) copy-start(f32[80]{0:T(128)} %param.9) | copy-start | bytes 964
  210.1 227.7 %all-gather.9.cloned.1.call-start = ((), (), s32[]{:S(2)}) async-start(), calls=%async_computation.5 | async-start | bytes 21626880 | tf_op jit(solution)/shard_map/all_gather | solution.py:11
  272.7 206.6 %reduce-scatter.2.cloned.1.call-start = ((), (), s32[]{:S(2)}) async-start(), calls=%async_computation.3 | async-start | bytes 4718592 | tf_op jit(solution)/shard_map/reduce_scatter | solution.py:64
Sparse Core Ops, SparseCore 0:
  9.2 33.6 all-gather.6
  45.5 139.2 all-gather.4
  210.2 62.3 all-reduce.2
  275.1 162.6 all-gather.8
  440.2 35.0 reduce-scatter.1
where the time goes:
time: 492 us; the launch traced here: 488 us
  waiting for transfers between devices  262 us (53%)
  blocking collectives  120 us (24%)
  matrix products  43.8 us (9%)
  other arithmetic  42.7 us (9%)
  between operations  13.9 us (3%)
  local copies, waits for them, and re-layouts  4.95 us (1%)
    all_gather x1, waiting for transfers between devices, per_device(): lax.all_gather(filter_mats, 'ctx', axis=1, tiled=True)  142 us
    unnamed x1, blocking collectives  120 us
    psum x1, waiting for transfers between devices, per_device(): pole_sum = lax.psum(stacked[length:], 'grp')  62.5 us
    select_n x32, other arithmetic, step(): return jax.tree.map(lambda a, b: jnp.where(reached, a, b), new, before)  39.9 us
    all_gather x1, waiting for transfers between devices, per_device(): full_grad = lax.all_gather(out_grad, 'grp', axis=1, tiled=True)  30.6 us
    all_gather x1, waiting for transfers between devices, entering(): everything = jax.tree.map(lambda part: lax.all_gather(part, axis), array)  25.1 us
    dot_general x1, matrix products, per_device(): jnp.einsum('kts,kti->si', kernel_mat, proj_grad, precision=exact_prec)  17.5 us
    dot_general x1, matrix products, per_device(): jnp.einsum('tj,kij->kti', full_grad, lax.all_gather(filter_mats, 'ctx', a...  12.9 us
  transfers between devices with their start and end apart: 5, of which 4 were waited for; matrix products, arithmetic and copies ran while one was open for 13% of the time, Pallas kernels for 0%

commit v1 on v0

v1 whole, which is shorter than its diff:
```python
import jax
import jax.numpy as jnp
from jax import lax
from jax.experimental import pallas as pl
from jax.experimental.pallas import tpu as pltpu
from jax.sharding import PartitionSpec as P

MESH = pl.DeviceIdType.MESH
F32, BF16 = jnp.float32, jnp.bfloat16
NX, NZ, NY = 4, 8, 4
TOK, WIDE, HALF, D = 512, 256, 1024, 2048
POLES, UNITS = 80, 24
HI = TOK
LO = TOK + POLES
ROWS = TOK + 2 * POLES
NT = (((1,), (1,)), ((), ()))
NN = (((1,), (0,)), ((), ()))


def split(value):
    high = value.astype(BF16)
    return high, (value - high.astype(F32)).astype(BF16)


def mm(a, b, dims=NN):
    return lax.dot_general(a, b, dims, preferred_element_type=F32)


def kernel(
    g_ref, m_ref, rates_col, rates_row, gains_row, coef_row, out_ref,
    grads, mats, kern_hi, kern_lo, proj_hi, proj_lo, parts, arrived, edge_hi, edge_lo,
    state_hi, state_lo, coef_col, unit_rates, unit_out, unit_in, total_out, total_in,
    enter_out, enter_in,
    g_send, g_recv, gs_send, gs_recv, m_send, m_recv, ms_send, ms_recv, u_send, u_recv,
    t_send, t_recv, e_send, e_recv, o_send, o_recv, l_sem,
):
    ctx, grp = lax.axis_index("ctx"), lax.axis_index("grp")
    x, z, y, c = ctx // NZ, ctx % NZ, grp // 2, grp % 2

    def device(x_to=None, z_to=None, y_to=None, c_to=None):
        pick = lambda new, own: own if new is None else new
        return (pick(x_to, x) * NZ + pick(z_to, z), pick(y_to, y) * 2 + pick(c_to, c))

    def remote(src, dst, send, recv, target):
        copy = pltpu.make_async_remote_copy(
            src_ref=src, dst_ref=dst, send_sem=send, recv_sem=recv,
            device_id=target, device_id_type=MESH,
        )
        return copy

    sibling = device(c_to=1 - c)
    slot = lambda x_of: (x_of + 4 - 2 * c) % NX
    col = lambda y_of: pl.ds(pl.multiple_of(c * HALF + y_of * WIDE, WIDE), WIDE)
    side = pl.ds(pl.multiple_of(c * HALF, HALF), HALF)
    pair_ks = pl.ds(2 * c, 2)

    barrier = pltpu.get_barrier_semaphore()
    partners = [device(z_to=(z + d) % NZ) for d in range(1, NZ)]
    partners += [device(x_to=(x + d) % NX) for d in range(1, NX)]
    partners += [device(y_to=(y + d) % NY) for d in range(1, NY)]
    partners += [sibling]
    for target in partners:
        pl.semaphore_signal(barrier, inc=1, device_id=target, device_id_type=MESH)
    for block in range(2):
        for half in range(2):
            own = jnp.logical_and(jnp.logical_and(2 * c + block == x, x == y), half == c)

            @pl.when(jnp.logical_not(own))
            def _():
                pl.semaphore_signal(
                    barrier, inc=1, device_id_type=MESH,
                    device_id=device(x_to=2 * c + block, y_to=x, c_to=half),
                )
    for y_of in range(NY):
        own = jnp.logical_and(jnp.logical_and(y == x, y_of == y), x // 2 == c)

        @pl.when(jnp.logical_not(own))
        def _():
            pl.semaphore_signal(
                barrier, inc=1, device_id_type=MESH,
                device_id=device(x_to=y, y_to=y_of, c_to=x // 2),
            )
    self_out = jnp.logical_and(x == y, x // 2 == c)

    low = pl.ds(pl.multiple_of(64 * (z % 2), 64), 64)
    for c_of in range(2):
        for y_of in range(NY):
            mats[z // 2, pair_ks, low, (c_of * NY + y_of) * WIDE : (c_of * NY + y_of + 1) * WIDE] = m_ref[
                :, :, (y_of * 2 + c_of) * WIDE : (y_of * 2 + c_of + 1) * WIDE
            ]
    own_copy = pltpu.make_async_copy(g_ref, grads.at[slot(x), 0:TOK, col(y)], l_sem.at[0])
    own_copy.start()

    rates_c = rates_col[0:96, :]
    state = jnp.zeros((96, WIDE), F32)
    for part in range(4):
        pos = lax.broadcasted_iota(jnp.int32, (96, 128), 1).astype(F32) + 128.0 * part
        dec_hi, dec_lo = split(jnp.exp(-pos * rates_c))
        rows = g_ref[128 * part : 128 * part + 128, :]
        state = state + mm(dec_hi, rows) + mm(dec_lo, rows)
    for group in range(12):
        for half in range(2):
            unit_out[group * 2 + half] = state[8 * group : 8 * group + 8, 128 * half : 128 * half + 128]
            unit_rates[group * 2 + half] = rates_col[8 * group : 8 * group + 8, :]

    pl.semaphore_wait(barrier, jnp.where(self_out, len(partners) + 6, len(partners) + 8))

    unit_copies = []
    for d in range(1, NZ):
        to = (z + d) % NZ
        copy = remote(
            unit_out.at[pl.ds(3 * to, 3)], unit_in.at[z], u_send.at[d], u_recv.at[d], device(z_to=to)
        )
        copy.start()
        unit_copies.append(copy)

    def piece(z_of, k):
        return mats.at[z_of // 2, 2 * c + k, pl.ds(pl.multiple_of(64 * (z_of % 2), 64), 64), :]

    m_wait, ms_wait = [], []

    def ring(d, k, way):
        z_of = (z + NZ - way * (d - 1)) % NZ
        ref = piece(z_of, k)
        i = ((d - 1) * 2 + k) * 2 + (way + 1) // 2
        copy = remote(ref, ref, m_send.at[i], m_recv.at[i], device(z_to=(z + NZ + way) % NZ))
        copy.start()
        m_wait.append(copy)
        return copy

    def arrive(copy, d, k, way):
        z_of = (z + NZ - way * d) % NZ
        ref = piece(z_of, k)
        i = ((d - 1) * 2 + k) * 2 + (way + 1) // 2
        copy.wait_recv()
        over = remote(ref, ref, ms_send.at[i], ms_recv.at[i], sibling)
        over.start()
        ms_wait.append(over)
        return over

    ring_copies = {}
    for k in range(2):
        for way in (1, -1):
            ring_copies[1, k, way] = ring(1, k, way)
    own_ref = mats.at[z // 2, pair_ks, low, :]
    own_over = remote(own_ref, own_ref, ms_send.at[16], ms_recv.at[16], sibling)
    own_over.start()

    over_copies = {}

    def event(d, k):
        for way in (1, -1):
            over_copies[d, k, way] = arrive(ring_copies[d, k, way], d, k, way)
            if d < 3 or (d == 3 and way == (1 if k == 0 else -1)):
                ring_copies[d + 1, k, way] = ring(d + 1, k, way)

    g_wait, gs_wait = [], []

    def send_g(base, i, src, dst, target):
        copy = remote(src, dst, g_send.at[base + i], g_recv.at[base + i], target)
        copy.start()
        g_wait.append(copy)
        return copy

    def over_g(base, i, src, dst):
        copy = remote(src, dst, gs_send.at[base + i], gs_recv.at[base + i], sibling)
        copy.start()
        gs_wait.append(copy)

    north = lambda d: (y + NY + d) % NY
    east = lambda d: (x + NX + d) % NX
    to_y = lambda d: device(y_to=north(d))
    to_x = lambda d: device(x_to=east(d))

    class YThenX:
        def __init__(self, n, row, size, cut):
            self.base, self.over = 8 * n, 4 * n
            self.rows = pl.ds(row, size)
            self.first, self.last = pl.ds(row, cut), pl.ds(row + cut, size - cut)

        def start(self, src):
            ref = grads.at[slot(x), self.rows, col(y)]
            src = ref if src is None else src
            self.a = send_g(self.base, 0, src, ref, to_y(1))
            self.b = send_g(self.base, 1, src, ref, to_y(-1))

        def relay(self):
            self.a.wait_recv()
            ref = grads.at[slot(x), self.first, col(north(-1))]
            self.d = send_g(self.base, 2, ref, ref, to_y(1))
            self.b.wait_recv()
            ref = grads.at[slot(x), self.last, col(north(1))]
            self.e = send_g(self.base, 3, ref, ref, to_y(-1))

        def turn(self):
            self.d.wait_recv()
            self.e.wait_recv()
            ref = grads.at[slot(x), self.rows, side]
            self.a = send_g(self.base, 4, ref, ref, to_x(1))
            self.b = send_g(self.base, 5, ref, ref, to_x(-1))

        def relay_again(self):
            self.a.wait_recv()
            ref = grads.at[slot(east(-1)), self.first, side]
            self.d = send_g(self.base, 6, ref, ref, to_x(1))
            self.b.wait_recv()
            ref = grads.at[slot(east(1)), self.last, side]
            self.e = send_g(self.base, 7, ref, ref, to_x(-1))
            mine = x // 2 == 1 - c
            opposite = east(2)
            buddy = lambda v: v + 1 - 2 * (v % 2)
            self.share(0, slot(jnp.where(mine, x, buddy(opposite))))
            self.second = slot(jnp.where(mine, buddy(x), opposite))

        def share(self, i, s):
            over_g(self.over, i, grads.at[s, self.rows, side], grads.at[s - 2, self.rows, side])

        def finish(self):
            self.d.wait_recv()
            self.e.wait_recv()
            self.share(1, self.second)

    class XThenY:
        def __init__(self, n, row, size, cut):
            self.base, self.over = 8 * n, 4 * n
            self.rows = pl.ds(row, size)
            self.first, self.last = pl.ds(row, cut), pl.ds(row + cut, size - cut)

        def start(self, src):
            ref = grads.at[slot(x), self.rows, col(y)]
            src = ref if src is None else src
            self.a = send_g(self.base, 0, src, ref, to_x(1))
            self.b = send_g(self.base, 1, src, ref, to_x(-1))

        def relay(self):
            self.a.wait_recv()
            ref = grads.at[slot(east(-1)), self.first, col(y)]
            self.d = send_g(self.base, 2, ref, ref, to_x(1))
            self.b.wait_recv()
            ref = grads.at[slot(east(1)), self.last, col(y)]
            self.e = send_g(self.base, 3, ref, ref, to_x(-1))

        def turn(self):
            self.d.wait_recv()
            self.e.wait_recv()
            ref = grads.at[:, self.rows, col(y)]
            self.a = send_g(self.base, 4, ref, ref, to_y(1))
            self.b = send_g(self.base, 5, ref, ref, to_y(-1))
            self.share(0, y)

        def relay_again(self):
            self.a.wait_recv()
            ref = grads.at[:, self.first, col(north(-1))]
            self.d = send_g(self.base, 6, ref, ref, to_y(1))
            self.b.wait_recv()
            ref = grads.at[:, self.last, col(north(1))]
            self.e = send_g(self.base, 7, ref, ref, to_y(-1))
            self.share(1, north(-1))
            self.share(2, north(1))

        def share(self, i, y_of):
            over_g(
                self.over, i, grads.at[2:4, self.rows, col(y_of)], grads.at[0:2, self.rows, col(y_of)]
            )

        def finish(self):
            self.d.wait_recv()
            self.e.wait_recv()
            self.share(3, north(2))

    tok_a, tok_b = YThenX(0, 0, 256, 128), XThenY(1, 256, 256, 128)
    ent_a, ent_b = YThenX(2, HI, POLES, 48), XThenY(3, LO, POLES, 48)

    tok_a.start(g_ref.at[0:256, :])
    tok_b.start(g_ref.at[256:512, :])

    own_units = pl.ds(3 * z, 3)
    lam = jnp.exp(-float(TOK) * unit_rates[own_units])
    unit_in[z] = unit_out[own_units]
    for copy in unit_copies:
        copy.wait_recv()
    run = jnp.zeros((3, 8, 128), F32)
    for z_of in range(NZ - 1, -1, -1):
        enter_out[z_of] = run
        run = unit_in[z_of] + lam * run
    total_out[...] = run
    total_in[x] = run
    total_copies = []
    for d in range(1, NX):
        copy = remote(
            total_out, total_in.at[x], t_send.at[d], t_recv.at[d], device(x_to=(x + d) % NX)
        )
        copy.start()
        total_copies.append(copy)

    tok_a.relay()
    tok_b.relay()

    rates_r = rates_row[0:1, :]
    rise_pos = lax.broadcasted_iota(jnp.int32, (TOK, 128), 0).astype(F32)
    falling = jnp.exp((rise_pos - 256.0) * rates_r)
    rising = jnp.exp((256.0 - rise_pos) * rates_r)
    edge = gains_row[0:1, :] * jnp.exp((rise_pos - float(TOK)) * rates_r)
    edge_hi[...], edge_lo[...] = split(edge)

    def taps(th, k):
        size = 256 * (th + 1)
        scaled = rising[256 * th : 256 * th + 256] * (coef_row[y, k : k + 1, :] * gains_row[0:1, :])
        mat = lax.dot_general(
            falling[0:size], scaled, NT, precision=lax.Precision.HIGHEST, preferred_element_type=F32
        )
        s_at = lax.broadcasted_iota(jnp.int32, (size, 256), 0)
        t_at = lax.broadcasted_iota(jnp.int32, (size, 256), 1) + 256 * th
        high, rest = split(jnp.where(t_at >= s_at, mat, 0.0))
        at = th * HALF + k * 256
        kern_hi[0:size, at : at + 256] = high
        kern_lo[0:size, at : at + 256] = rest

    for k in range(4):
        taps(0, k)
    own_copy.wait()
    tok_a.turn()
    tok_b.turn()
    event(1, 0)

    for copy in total_copies:
        copy.wait_recv()
    lam_row = jnp.exp(-float(TOK * NZ) * unit_rates[own_units])
    carry = jnp.zeros((3, 8, 128), F32)
    for x_of in range(NX - 1, 0, -1):
        carry = jnp.where(x_of > x, total_in[x_of] + lam_row * carry, carry)
    for z_of in range(NZ - 1, -1, -1):
        enter_out[z_of] = enter_out[z_of] + carry
        carry = lam * carry
    enter_copies = []
    for d in range(1, NZ):
        to = (z + d) % NZ
        copy = remote(
            enter_out.at[to], enter_in.at[own_units], e_send.at[d], e_recv.at[d], device(z_to=to)
        )
        copy.start()
        enter_copies.append(copy)
    enter_in[own_units] = enter_out[z]

    for k in range(4):
        taps(1, k)
        coef_col[k] = jnp.broadcast_to(coef_row[y, k : k + 1, :], (128, 128)).T
    state_hi[...] = jnp.zeros_like(state_hi)
    state_lo[...] = jnp.zeros_like(state_lo)
    event(1, 1)
    for d in range(1, NZ):
        source = (z + NZ - d) % NZ
        remote(
            enter_out.at[0], enter_in.at[pl.ds(3 * source, 3)], e_send.at[d], e_recv.at[d], sibling
        ).wait_recv()
    for group in range(10):
        for half in range(2):
            high, rest = split(enter_in[group * 2 + half])
            grads_cols = pl.ds(pl.multiple_of(c * HALF + y * WIDE + 128 * half, 128), 128)
            grads[slot(x), HI + 8 * group : HI + 8 * group + 8, grads_cols] = high
            grads[slot(x), LO + 8 * group : LO + 8 * group + 8, grads_cols] = rest
    ent_a.start(None)
    ent_b.start(None)
    tok_a.relay_again()
    tok_b.relay_again()
    event(2, 0)
    ent_a.relay()
    ent_b.relay()
    tok_a.finish()
    tok_b.finish()
    ent_a.turn()
    ent_b.turn()
    event(2, 1)

    def near(q):
        filters = mats.at[q]

        @pl.loop(0, 4)
        def _(step):
            block, th = step // 2, step % 2
            rows = grads[block, pl.ds(pl.multiple_of(th * 256, 256), 256), :]
            for k in range(4):
                high, rest = split(mm(rows, filters[k], NT))
                at = pl.ds(pl.multiple_of(th * HALF + k * 256, 256), 256)
                lanes = pl.ds(pl.multiple_of(block * 128, 128), 128)
                proj_hi[at, lanes] = high
                proj_lo[at, lanes] = rest

        for sh in range(2):
            s_rows, t_rows = slice(256 * sh, 256 * sh + 256), slice(HALF * sh, D)
            acc = (
                mm(kern_hi[s_rows, t_rows], proj_hi[t_rows, :])
                + mm(kern_hi[s_rows, t_rows], proj_lo[t_rows, :])
                + mm(kern_lo[s_rows, t_rows], proj_hi[t_rows, :])
            )
            parts[q, 0, s_rows, :] = acc[:, 0:128]
            parts[q, 1, s_rows, :] = acc[:, 128:256]

    out_waits = []

    def far(n, q):
        for block in range(2):
            total = jnp.zeros((POLES, 128), F32)
            for k in range(4):
                both = mm(grads[block, HI:ROWS, :], mats[q, k], NT)
                total = total + coef_col[k, 0:POLES, :] * (both[0:POLES] + both[POLES : 2 * POLES])
            high, rest = split(total)
            state_hi[0:POLES, 128 * block : 128 * block + 128] = high
            state_lo[0:POLES, 128 * block : 128 * block + 128] = rest
        acc = (
            mm(edge_hi[...], state_hi[...])
            + mm(edge_hi[...], state_lo[...])
            + mm(edge_lo[...], state_hi[...])
        )
        for block in range(2):
            parts[q, block] = parts[q, block] + acc[:, 128 * block : 128 * block + 128]
            own = jnp.logical_and(jnp.logical_and(2 * c + block == x, x == y), q // 2 == c)
            cols = pl.ds(pl.multiple_of((q % 2) * 128, 128), 128)
            i = 2 * n + block
            away = remote(
                parts.at[q, block], arrived.at[y, :, cols], o_send.at[i], o_recv.at[y, q % 2],
                device(x_to=2 * c + block, y_to=x, c_to=q // 2),
            )
            local = pltpu.make_async_copy(
                parts.at[q, block], arrived.at[y, :, cols], o_recv.at[y, q % 2]
            )

            @pl.when(jnp.logical_not(own))
            def _():
                away.start()

            @pl.when(own)
            def _():
                local.start()

            out_waits.append((own, away))

    def over_in(d, k):
        for way in (1, -1):
            if (d, k, way) in over_copies:
                over_copies[d, k, way].wait_recv()

    def last_event():
        for k, way in ((0, 1), (1, -1)):
            over_copies[4, k, way] = arrive(ring_copies[4, k, way], 4, k, way)

    q_own = z // 2
    lean = 1 - 2 * (z % 2)
    order = [q_own, (q_own + 4 - lean) % 4, (q_own + 4 + lean) % 4, (q_own + 2) % 4]

    def g_over_in(lo, hi):
        for copy in gs_wait[lo:hi]:
            copy.wait_recv()

    own_over.wait_recv()
    over_in(1, 0)
    over_in(1, 1)
    shared = len(gs_wait)
    g_over_in(0, shared)
    near(order[0])
    event(3, 0)
    ent_a.relay_again()
    ent_b.relay_again()
    over_in(2, 0)
    over_in(2, 1)
    near(order[1])
    ent_a.finish()
    ent_b.finish()
    event(3, 1)
    g_over_in(shared, len(gs_wait))
    far(0, order[0])
    far(1, order[1])
    over_in(3, 0)
    over_in(3, 1)
    near(order[2])
    far(2, order[2])
    last_event()
    over_in(4, 0)
    over_in(4, 1)
    near(order[3])
    far(3, order[3])

    for y_of in range(NY):
        for half in range(2):
            ref = arrived.at[y_of, :, 128 * half : 128 * half + 128]
            pltpu.make_async_copy(ref, ref, o_recv.at[y_of, half]).wait()
    out_ref[...] = (arrived[0] + arrived[1] + arrived[2] + arrived[3]).astype(BF16)

    for copy in unit_copies + total_copies + enter_copies + m_wait + ms_wait + g_wait + gs_wait + [own_over]:
        copy.wait_send()
    for own, away in out_waits:

        @pl.when(jnp.logical_not(own))
        def _():
            away.wait_send()


def per_device(out_grad, filter_mats, coeffs, pole_rates):
    rates = jnp.pad(pole_rates, (0, 128 - POLES))
    gains = jnp.sqrt(-jnp.expm1(-2.0 * rates))
    rates_col = jnp.broadcast_to(rates[:, None], (128, 128))
    rates_row = jnp.broadcast_to(rates[None, :], (8, 128))
    gains_row = jnp.broadcast_to(gains[None, :], (8, 128))
    coef_row = jnp.pad(coeffs, ((0, 0), (0, 128 - POLES))).reshape(4, 4, 128)
    dma = pltpu.SemaphoreType.DMA
    vmem = pl.BlockSpec(memory_space=pltpu.VMEM)
    return pl.pallas_call(
        kernel,
        out_shape=jax.ShapeDtypeStruct((TOK, WIDE), BF16),
        in_specs=[vmem] * 6,
        out_specs=vmem,
        scratch_shapes=[
            pltpu.VMEM((NX, ROWS, D), BF16),
            pltpu.VMEM((4, 4, 128, D), BF16),
            pltpu.VMEM((TOK, D), BF16),
            pltpu.VMEM((TOK, D), BF16),
            pltpu.VMEM((D, 256), BF16),
            pltpu.VMEM((D, 256), BF16),
            pltpu.VMEM((4, 2, TOK, 128), F32),
            pltpu.VMEM((NY, TOK, WIDE), F32),
            pltpu.VMEM((TOK, 128), BF16),
            pltpu.VMEM((TOK, 128), BF16),
            pltpu.VMEM((128, 256), BF16),
            pltpu.VMEM((128, 256), BF16),
            pltpu.VMEM((4, 128, 128), F32),
            pltpu.VMEM((UNITS, 8, 128), F32),
            pltpu.VMEM((UNITS, 8, 128), F32),
            pltpu.VMEM((NZ, 3, 8, 128), F32),
            pltpu.VMEM((3, 8, 128), F32),
            pltpu.VMEM((NX, 3, 8, 128), F32),
            pltpu.VMEM((NZ, 3, 8, 128), F32),
            pltpu.VMEM((UNITS, 8, 128), F32),
            dma((32,)), dma((32,)), dma((16,)), dma((16,)),
            dma((16,)), dma((16,)), dma((17,)), dma((17,)),
            dma((NZ,)), dma((NZ,)), dma((NX,)), dma((NX,)), dma((NZ,)), dma((NZ,)),
            dma((8,)), dma((NY, 2)), dma((1,)),
        ],
        compiler_params=pltpu.CompilerParams(
            collective_id=0, has_side_effects=True, vmem_limit_bytes=60 * 1024 * 1024
        ),
        name="spectral_grad",
    )(out_grad, filter_mats, rates_col, rates_row, gains_row, coef_row)


def solution(mesh):
    placed = (P("ctx", "grp"), P("grp", "ctx", None), P(), P())
    return jax.shard_map(
        per_device, mesh=mesh, in_specs=placed, out_specs=P("ctx", "grp"), check_vma=False
    )
```

time: 492 us -> 98.6 us (0.20)
  waiting for transfers between devices: 262 us -> 0 us
  blocking collectives: 120 us -> 0 us
  Pallas kernels: 0 us -> 93.5 us
  matrix products: 43.8 us -> 0 us
  other arithmetic: 42.7 us -> 0.68 us
  between operations: 13.9 us -> 0.01 us
    all_gather x3 -> x0, waiting for transfers between devices: 198 us -> none  [the longest x1 142 us: per_device(): lax.all_gather(filter_mats, 'ctx', axis=1, tiled=True)]
    unnamed x1 -> x0, blocking collectives: 120 us -> none
    pallas_call x0 -> x1, Pallas kernels: none -> 93.5 us  [per_device(): pl.pallas_call(kernel, out_shape=jax.ShapeDtypeStruct((TOK, WIDE), BF16),...]
    psum x1 -> x0, waiting for transfers between devices: 62.5 us -> none  [per_device(): pole_sum = lax.psum(stacked[length:], 'grp')]
    dot_general x5 -> x0, matrix products: 43.8 us -> none  [the longest x1 17.5 us: per_device(): jnp.einsum('kts,kti->si', kernel_mat, proj_grad, precision=exact_prec)]
    select_n x32 -> x0, other arithmetic: 39.9 us -> none  [step(): return jax.tree.map(lambda a, b: jnp.where(reached, a, b), new, before)]
  transfers between devices with their start and end apart: 5 -> 0, of which waited for: 4 -> 0; matrix products, arithmetic and copies ran while one was open for 13% -> 0% of each run, Pallas kernels for 0% -> 0%
where the time goes in v1:
time: 98.6 us; the launch traced here: 98.4 us
  Pallas kernels  93.5 us (95%)
  local copies, waits for them, and re-layouts  4.19 us (4%)
    pallas_call x1, Pallas kernels, per_device(): pl.pallas_call(kernel, out_shape=jax.ShapeDtypeStruct((TOK, WIDE), BF16),...  93.5 us

profile of v1, /device:TPU:1, one launch (start us, length us, event | category | flops | bytes accessed | tf_op | source)
XLA Modules:
  0.0 98.4 jit_solution(16033758801140898729)
XLA Ops:
  0.0 0.0 copy-start
  0.0 0.7 negate_sqrt_fusion
  0.7 0.6 broadcast_in_dim.8.gains_row
  1.3 0.6 broadcast_in_dim.7.rates_row
  1.9 0.0 copy-done
  1.9 0.6 pad.9
  2.5 0.7 broadcast_in_dim.6.rates_col
  3.2 93.5 %spectral_grad.1 = bf16[512,256]{1,0:T(8,128)(2,1)} custom-call(bf16[512,256]{1,0:T(8,128)(2,1)} %g_ref.1, bf16[2,64,2048]{2,1,0:T(8,128)(2,1)} %m_ref.1, f32[128,128]{1,0:T(8,128)} %broadcast_in_dim.6.rates_col, f32[8,128]{1,0:T(8,128)} %broadcast_in_dim.7.rates_row, f32[8,128]{1,0:T(8,128)} %broadcast_in_dim.8.gains_row, f32[4,4,128]{2,1,0:T(4,128)} %bitcast.1), custom_call_target="tpu_custom_call" | custom-call | tf_op jit(solution)/shard_map/spectral_grad/pallas_call | solution.py:507
  96.7 1.7 %copy.6 = bf16[512,256]{1,0:T(8,128)(2,1)} copy(bf16[512,256]{1,0:T(8,128)(2,1)} %spectral_grad.1) | data formatting | bytes 524288
Async XLA Ops:
  0.0 1.9 %copy-start = (f32[16,80]{1,0:T(8,128)S(1)}, f32[16,80]{1,0:T(8,128)}, u32[]{:S(2)}) copy-start(f32[16,80]{1,0:T(8,128)} %param.6) | copy-start | bytes 15364

commit v2 on v0

v2 whole, which is shorter than its diff:
```python
import jax
import jax.numpy as jnp
from jax import lax
from jax.experimental import pallas as pl
from jax.experimental.pallas import tpu as pltpu
from jax.sharding import PartitionSpec as P

MESH = pl.DeviceIdType.MESH
F32, BF16 = jnp.float32, jnp.bfloat16
NX, NZ, NY = 4, 8, 4
TOK, WIDE, HALF, D = 512, 256, 1024, 2048
POLES, UNITS = 80, 24
HI = TOK
LO = TOK + POLES
ROWS = TOK + 2 * POLES
NT = (((1,), (1,)), ((), ()))
NN = (((1,), (0,)), ((), ()))
OFFSETS = (0, -1, 1, 2)


def split(value):
    high = value.astype(BF16)
    return high, (value - high.astype(F32)).astype(BF16)


def mm(a, b, dims=NN):
    return lax.dot_general(a, b, dims, preferred_element_type=F32)


def minus_expm1_neg(u):
    series = jnp.ones_like(u)
    for n in range(9, 1, -1):
        series = 1.0 - u * (1.0 / n) * series
    return jnp.where(u < 0.25, u * series, 1.0 - jnp.exp(-u))


def kernel(
    g_ref, m_ref, rates_ref, coeffs_ref, out_ref,
    grads, mats, kern_hi, kern_lo, proj_hi, proj_lo, parts, arrived, edge_hi, edge_lo,
    state_hi, state_lo, coef_col, rates_row, coef_row, rates_col, unit_rates, unit_out, unit_in,
    total_out, total_in, enter_out, enter_in,
    p1_send, p1_recv, p2_send, p2_recv, rl_send, rl_recv, sh_send, sh_recv,
    g_send, g_recv, m_send, m_recv, ms_send, ms_recv, u_send, u_recv,
    t_send, t_recv, e_send, e_recv, o_send, o_recv, l_sem,
):
    ctx, grp = lax.axis_index("ctx"), lax.axis_index("grp")
    x, z, y, c = ctx // NZ, ctx % NZ, grp // 2, grp % 2

    def device(x_to=None, z_to=None, y_to=None, c_to=None):
        pick = lambda new, own: own if new is None else new
        return (pick(x_to, x) * NZ + pick(z_to, z), pick(y_to, y) * 2 + pick(c_to, c))

    def remote(src, dst, send, recv, target):
        copy = pltpu.make_async_remote_copy(
            src_ref=src, dst_ref=dst, send_sem=send, recv_sem=recv,
            device_id=target, device_id_type=MESH,
        )
        return copy

    sibling = device(c_to=1 - c)
    slot = lambda x_of: (x_of + 4 - 2 * c) % NX
    col = lambda y_of: pl.ds(pl.multiple_of(c * HALF + y_of * WIDE, WIDE), WIDE)
    side = pl.ds(pl.multiple_of(c * HALF, HALF), HALF)

    barrier = pltpu.get_barrier_semaphore()
    partners = [device(z_to=(z + d) % NZ) for d in range(1, NZ)]
    partners += [device(x_to=(x + d) % NX) for d in range(1, NX)]
    partners += [device(y_to=(y + d) % NY) for d in range(1, NY)]
    partners += [sibling]
    for target in partners:
        pl.semaphore_signal(barrier, inc=1, device_id=target, device_id_type=MESH)
    for block in range(2):
        for half in range(2):
            own = jnp.logical_and(jnp.logical_and(2 * c + block == x, x == y), half == c)

            @pl.when(jnp.logical_not(own))
            def _():
                pl.semaphore_signal(
                    barrier, inc=1, device_id_type=MESH,
                    device_id=device(x_to=2 * c + block, y_to=x, c_to=half),
                )
    for y_of in range(NY):
        own = jnp.logical_and(jnp.logical_and(y == x, y_of == y), x // 2 == c)

        @pl.when(jnp.logical_not(own))
        def _():
            pl.semaphore_signal(
                barrier, inc=1, device_id_type=MESH,
                device_id=device(x_to=y, y_to=y_of, c_to=x // 2),
            )
    self_out = jnp.logical_and(x == y, x // 2 == c)

    low = pl.ds(pl.multiple_of(64 * (z % 2), 64), 64)
    for c_of in range(2):
        for y_of in range(NY):
            mats[z // 2, :, c, low, (c_of * NY + y_of) * WIDE : (c_of * NY + y_of + 1) * WIDE] = m_ref[
                :, :, (y_of * 2 + c_of) * WIDE : (y_of * 2 + c_of + 1) * WIDE
            ]
    own_copy = pltpu.make_async_copy(g_ref, grads.at[slot(x), 0:TOK, col(y)], l_sem.at[0])
    own_copy.start()

    rates_row[...] = jnp.zeros_like(rates_row)
    coef_row[...] = jnp.zeros_like(coef_row)
    rates_row[0:1, 0:POLES] = rates_ref[...]
    coef_row[:, 0:POLES] = coeffs_ref[...]
    rates_col[...] = jnp.broadcast_to(rates_row[0:1, :], (128, 128)).T
    gains = jnp.sqrt(minus_expm1_neg(2.0 * rates_row[0:1, :]))
    rates_c = rates_col[0:POLES, :]
    state = jnp.zeros((POLES, WIDE), F32)
    for part in range(4):
        pos = lax.broadcasted_iota(jnp.int32, (POLES, 128), 1).astype(F32) + 128.0 * part
        dec_hi, dec_lo = split(jnp.exp(-pos * rates_c))
        rows = g_ref[128 * part : 128 * part + 128, :]
        state = state + mm(dec_hi, rows) + mm(dec_lo, rows)
    for group in range(10):
        for half in range(2):
            unit_out[group * 2 + half] = state[8 * group : 8 * group + 8, 128 * half : 128 * half + 128]
            unit_rates[group * 2 + half] = rates_col[8 * group : 8 * group + 8, :]

    pl.semaphore_wait(barrier, jnp.where(self_out, len(partners) + 6, len(partners) + 8))

    unit_copies = []
    for d in range(1, NZ):
        to = (z + d) % NZ
        copy = remote(
            unit_out.at[pl.ds(3 * to, 3)], unit_in.at[z], u_send.at[d], u_recv.at[d], device(z_to=to)
        )
        copy.start()
        unit_copies.append(copy)

    g_wait, sent = [], []

    def send_g(i, j, src, dst, target):
        copy = remote(src, dst, g_send.at[i], g_recv.at[j], target)
        copy.start()
        g_wait.append(copy)

    north = lambda d: (y + NY + d) % NY
    east = lambda d: (x + NX + d) % NX
    to_y = lambda d: device(y_to=north(d))
    to_x = lambda d: device(x_to=east(d))

    hi_rows, lo_rows = pl.ds(HI, POLES), pl.ds(LO, POLES)

    def states_first():
        for d in range(1, 4):
            ref = grads.at[slot(x), hi_rows, col(y)]
            send_g(d - 1, d - 1, ref, ref, to_y(d))
            ref = grads.at[slot(x), lo_rows, col(y)]
            send_g(3 + d - 1, 3 + d - 1, ref, ref, to_x(d))

    def states_second():
        for copy in g_wait[0:6]:
            copy.wait_recv()
        ref, dst = grads.at[slot(x), hi_rows, side], grads.at[x % 2, hi_rows, side]
        for d in range(1, 4):
            send_g(6 + d - 1, 6 + 2 * (x % 2) + c, ref, dst, device(x_to=east(d), c_to=x // 2))
        hi_over = remote(ref, dst, g_send.at[9], g_recv.at[6 + 2 * (x % 2) + c], sibling)

        @pl.when(x // 2 != c)
        def _():
            hi_over.start()

        dst = grads.at[0:2, lo_rows, col(y)]
        away = grads.at[2:4, lo_rows, col(y)]
        for d in range(1, 4):
            send_g(9 + d, 10 + 2 * y + c, dst, dst, to_y(d))
            send_g(12 + d, 10 + 2 * y + c, away, dst, device(y_to=north(d), c_to=1 - c))
        send_g(16, 10 + 2 * y + c, away, dst, sibling)
        return hi_over

    def states_finish():
        ref = grads.at[0, hi_rows, side]
        for b in range(2):
            for c_of in range(2):

                @pl.when(jnp.logical_not(jnp.logical_and(2 * c + b == x, c_of == c)))
                def _():
                    remote(ref, ref, g_send.at[0], g_recv.at[6 + 2 * b + c_of], sibling).wait_recv()

        ref2 = grads.at[0:2, lo_rows, col(y)]
        for y_of in range(NY):
            for c_of in range(2):

                @pl.when(jnp.logical_not(jnp.logical_and(y_of == y, c_of == c)))
                def _():
                    remote(ref2, ref2, g_send.at[0], g_recv.at[10 + 2 * y_of + c_of], sibling).wait_recv()

    class Tokens:
        def __init__(self, n, row, y_first):
            self.n, self.y_first = n, y_first
            self.rows, self.first, self.last = pl.ds(row, 256), pl.ds(row, 128), pl.ds(row + 128, 128)
            self.src = g_ref.at[row : row + 256, :]
            self.hop1, self.hop2 = (to_y, to_x) if y_first else (to_x, to_y)
            self.p1, self.p2, self.shares = {}, {}, []

        def ref(self, d1, d2, rows, s=None):
            dx, dy = (d2, d1) if self.y_first else (d1, d2)
            return grads.at[slot(east(dx)) if s is None else s, rows, col(north(dy))]

        def copy(self, src, dst, i, target, first=True):
            send, recv = (p1_send, p1_recv) if first else (p2_send, p2_recv)
            copy = remote(src, dst, send.at[self.n, i], recv.at[self.n, i], target)
            copy.start()
            sent.append(copy)
            return copy

        def onward(self, j, src=None):
            ref = self.ref(OFFSETS[j], 0, self.rows)
            for way in (1, -1):
                self.p2[j, way] = self.copy(
                    ref if src is None else src, ref, 2 * j + (way + 1) // 2, self.hop2(way), False
                )

        def start(self):
            ref = self.ref(0, 0, self.rows)
            self.p1[0] = self.copy(self.src, ref, 0, self.hop1(1))
            self.p1[1] = self.copy(self.src, ref, 1, self.hop1(-1))

        def mid(self):
            for i, way, rows in ((0, 1, self.first), (1, -1, self.last)):
                self.p1[i].wait_recv()
                ref = self.ref(-way, 0, rows)
                self.p1[i + 2] = self.copy(ref, ref, i + 2, self.hop1(way))

        def opposite(self):
            self.p1[2].wait_recv()
            self.p1[3].wait_recv()
            self.onward(3)

        def relay(self, j):
            for way, rows in ((1, self.first), (-1, self.last)):
                self.p2[j, way].wait_recv()
                owner = east(-way) if self.y_first else east(OFFSETS[j])
                at = 8 * c + 2 * j + (way + 1) // 2 if self.y_first else 4 * c + 2 * (owner % 2) + (way + 1) // 2
                target = (
                    device(x_to=east(way), c_to=owner // 2)
                    if self.y_first
                    else device(y_to=north(way), c_to=owner // 2)
                )
                copy = remote(
                    self.ref(OFFSETS[j], -way, rows), self.ref(OFFSETS[j], -way, rows, owner % 2),
                    rl_send.at[self.n, 2 * j + (way + 1) // 2], rl_recv.at[self.n, at], target,
                )
                copy.start()
                sent.append(copy)

        def share_copy(self, i, src, dst):
            return remote(src, dst, sh_send.at[self.n, i], sh_recv.at[self.n, i], sibling)

        def share(self):
            if self.y_first:
                mine = x // 2 == 1 - c
                buddy = lambda v: v + 1 - 2 * (v % 2)
                s0 = slot(jnp.where(mine, x, buddy(east(2))))
                s1 = slot(jnp.where(mine, buddy(x), x))
                at = lambda s: grads.at[s, self.rows, side]
                copy = self.share_copy(0, at(s0), at(s0 - 2))
                copy.start()
                sent.append(copy)
                self.shares.append(copy)
                self.extra = self.share_copy(1, at(jnp.where(mine, s1, 2)), at(jnp.where(mine, s1 - 2, 0)))

                @pl.when(mine)
                def _():
                    self.extra.start()
            else:
                for i, dy in enumerate((0, -1, 1)):
                    at = lambda lo: grads.at[lo : lo + 2, self.rows, col(north(dy))]
                    copy = self.share_copy(i, at(2), at(0))
                    copy.start()
                    sent.append(copy)
                    self.shares.append(copy)

        def finish(self):
            for copy in self.shares:
                copy.wait_recv()
            piece_ref = grads.at[0, self.first, 0:WIDE]

            def wait_relays(count):
                for at in range(count):
                    remote(
                        piece_ref, piece_ref, rl_send.at[self.n, 0], rl_recv.at[self.n, at], sibling
                    ).wait_recv()

            if self.y_first:

                @pl.when(x // 2 == c)
                def _():
                    self.extra.wait_recv()

                @pl.when(east(2) // 2 == c)
                def _():
                    wait_relays(16)
            else:
                wait_relays(8)

        def drain(self):
            if self.y_first:

                @pl.when(x // 2 == 1 - c)
                def _():
                    self.extra.wait_send()

    tok_a, tok_b = Tokens(0, 0, True), Tokens(1, 256, False)

    tok_a.start()
    tok_b.start()
    tok_a.onward(0, tok_a.src)
    tok_b.onward(0, tok_b.src)

    def piece(z_of, d, k, way):
        start, size = 64 * (z_of % 2), 64
        if d == 4:
            start, size = start + 16 * (1 - way), 32
        return mats.at[z_of // 2, k, c, pl.ds(pl.multiple_of(start, 32), size), :]

    m_wait, ms_wait = [], []

    def ring(d, k, way):
        z_of = (z + NZ - way * (d - 1)) % NZ
        ref = piece(z_of, d, k, way)
        i = ((d - 1) * 2 + k) * 2 + (way + 1) // 2
        copy = remote(ref, ref, m_send.at[i], m_recv.at[i], device(z_to=(z + NZ + way) % NZ))
        copy.start()
        m_wait.append(copy)
        return copy

    def arrive(copy, d, k, way):
        z_of = (z + NZ - way * d) % NZ
        ref = piece(z_of, d, k, way)
        i = ((d - 1) * 2 + k) * 2 + (way + 1) // 2
        copy.wait_recv()
        over = remote(ref, ref, ms_send.at[i], ms_recv.at[i], sibling)
        over.start()
        ms_wait.append(over)
        return over

    ring_copies = {}
    for k in range(2):
        for way in (1, -1):
            ring_copies[1, k, way] = ring(1, k, way)
    own_ref = mats.at[z // 2, :, c, low, :]
    own_over = remote(own_ref, own_ref, ms_send.at[16], ms_recv.at[16], sibling)
    own_over.start()

    over_copies = {}

    def event(d, k):
        for way in (1, -1):
            over_copies[d, k, way] = arrive(ring_copies[d, k, way], d, k, way)
            if d < 4:
                ring_copies[d + 1, k, way] = ring(d + 1, k, way)

    own_units = pl.ds(3 * z, 3)
    total_copies, enter_copies = [], []

    def hand_on():
        lam = jnp.exp(-float(TOK) * unit_rates[own_units])
        unit_in[z] = unit_out[own_units]
        for copy in unit_copies:
            copy.wait_recv()
        run = jnp.zeros((3, 8, 128), F32)
        for z_of in range(NZ - 1, -1, -1):
            enter_out[z_of] = run
            run = unit_in[z_of] + lam * run
        total_out[...] = run
        total_in[x] = run
        for d in range(1, NX):
            copy = remote(
                total_out, total_in.at[x], t_send.at[d], t_recv.at[d], device(x_to=(x + d) % NX)
            )
            copy.start()
            total_copies.append(copy)

    def send_enter():
        for copy in total_copies:
            copy.wait_recv()
        lam_row = jnp.exp(-float(TOK * NZ) * unit_rates[own_units])
        carry = jnp.zeros((3, 8, 128), F32)
        for x_of in range(NX - 1, 0, -1):
            carry = jnp.where(x_of > x, total_in[x_of] + lam_row * carry, carry)
        lam = jnp.exp(-float(TOK) * unit_rates[own_units])
        for z_of in range(NZ - 1, -1, -1):
            enter_out[z_of] = enter_out[z_of] + carry
            carry = lam * carry
        for d in range(1, NZ):
            to = (z + d) % NZ
            copy = remote(
                enter_out.at[to], enter_in.at[own_units], e_send.at[d], e_recv.at[d], device(z_to=to)
            )
            copy.start()
            enter_copies.append(copy)
        enter_in[own_units] = enter_out[z]

    def store_enter():
        for d in range(1, NZ):
            source = (z + NZ - d) % NZ
            remote(
                enter_out.at[0], enter_in.at[pl.ds(3 * source, 3)], e_send.at[d], e_recv.at[d], sibling
            ).wait_recv()
        for group in range(10):
            for half in range(2):
                high, rest = split(enter_in[group * 2 + half])
                grads_cols = pl.ds(pl.multiple_of(c * HALF + y * WIDE + 128 * half, 128), 128)
                grads[slot(x), HI + 8 * group : HI + 8 * group + 8, grads_cols] = high
                grads[slot(x), LO + 8 * group : LO + 8 * group + 8, grads_cols] = rest

    rates_r = rates_row[0:1, :]
    rise_pos = lax.broadcasted_iota(jnp.int32, (TOK, 128), 0).astype(F32)
    falling = jnp.exp((rise_pos - 256.0) * rates_r)
    rising = jnp.exp((256.0 - rise_pos) * rates_r)
    edge = gains * jnp.exp((rise_pos - float(TOK)) * rates_r)
    edge_hi[...], edge_lo[...] = split(edge)

    def taps(th, k):
        size = 256 * (th + 1)
        scaled = rising[256 * th : 256 * th + 256] * (coef_row[pl.ds(4 * y + k, 1), :] * gains)
        mat = lax.dot_general(
            falling[0:size], scaled, NT, precision=lax.Precision.HIGHEST, preferred_element_type=F32
        )
        s_at = lax.broadcasted_iota(jnp.int32, (size, 256), 0)
        t_at = lax.broadcasted_iota(jnp.int32, (size, 256), 1) + 256 * th
        high, rest = split(jnp.where(t_at >= s_at, mat, 0.0))
        at = (k % 2) * HALF + th * TOK + (k // 2) * 256
        kern_hi[0:size, at : at + 256] = high
        kern_lo[0:size, at : at + 256] = rest

    def more_taps(ks):
        for k in ks:
            taps(1, k)
            coef_col[k] = jnp.broadcast_to(coef_row[pl.ds(4 * y + k, 1), :], (128, 128)).T

    tok_a.mid()
    tok_b.mid()
    hand_on()
    for j in (1, 2):
        tok_a.onward(j)
        tok_b.onward(j)
    for k in range(4):
        taps(0, k)
    own_copy.wait()
    tok_a.opposite()
    tok_b.opposite()
    send_enter()
    event(1, 0)
    tok_a.relay(0)
    tok_b.relay(0)
    more_taps((0, 1))
    tok_a.relay(1)
    tok_b.relay(1)
    event(1, 1)
    tok_a.relay(2)
    tok_b.relay(2)
    state_hi[...] = jnp.zeros_like(state_hi)
    state_lo[...] = jnp.zeros_like(state_lo)
    store_enter()
    states_first()
    tok_a.relay(3)
    tok_b.relay(3)
    tok_a.share()
    tok_b.share()
    more_taps((2,))
    event(2, 0)
    more_taps((3,))

    def project(q, kk):
        weights = mats[q, kk].reshape(256, D)
        parts_of = [(block, th) for block in range(2) for th in range(2)]
        tiles = [mm(grads[block, 256 * th : 256 * th + 256, :], weights, NT) for block, th in parts_of]
        for (block, th), tile in zip(parts_of, tiles):
            high, rest = split(tile)
            for c_of in range(2):
                at = kk * HALF + th * TOK + c_of * 256
                lanes, own = slice(128 * block, 128 * block + 128), slice(128 * c_of, 128 * c_of + 128)
                proj_hi[at : at + 256, lanes] = high[:, own]
                proj_lo[at : at + 256, lanes] = rest[:, own]

    def near(sh, kk):
        s_rows = slice(256 * sh, 256 * sh + 256)
        t_rows = slice(HALF * kk + TOK * sh, HALF * kk + HALF)
        return (
            mm(kern_hi[s_rows, t_rows], proj_hi[t_rows, :])
            + mm(kern_hi[s_rows, t_rows], proj_lo[t_rows, :])
            + mm(kern_lo[s_rows, t_rows], proj_hi[t_rows, :])
        )

    def enter(q):
        both = mm(grads[0:2, HI:ROWS, :].reshape(4 * POLES, D), mats[q].reshape(512, D), NT)
        for block in range(2):
            total = jnp.zeros((POLES, 128), F32)
            top = 2 * POLES * block
            for kk in range(2):
                for c_of in range(2):
                    at = 256 * kk + 128 * c_of
                    lanes = slice(at, at + 128)
                    total = total + coef_col[2 * c_of + kk, 0:POLES, :] * (
                        both[top : top + POLES, lanes] + both[top + POLES : top + 2 * POLES, lanes]
                    )
            high, rest = split(total)
            state_hi[0:POLES, 128 * block : 128 * block + 128] = high
            state_lo[0:POLES, 128 * block : 128 * block + 128] = rest

    def far(sh):
        s_rows = slice(256 * sh, 256 * sh + 256)
        return (
            mm(edge_hi[s_rows, :], state_hi[...])
            + mm(edge_hi[s_rows, :], state_lo[...])
            + mm(edge_lo[s_rows, :], state_hi[...])
        )

    out_waits = []

    def deliver(n, q, sh):
        s_rows = slice(256 * sh, 256 * sh + 256)
        for block in range(2):
            own = jnp.logical_and(jnp.logical_and(2 * c + block == x, x == y), q // 2 == c)
            cols = pl.ds(pl.multiple_of((q % 2) * 128, 128), 128)
            src, dst = parts.at[n, block, s_rows, :], arrived.at[y, s_rows, cols]
            done = o_recv.at[y, 2 * (q % 2) + sh]
            away = remote(
                src, dst, o_send.at[4 * n + 2 * block + sh], done,
                device(x_to=2 * c + block, y_to=x, c_to=q // 2),
            )
            local = pltpu.make_async_copy(src, dst, done)

            @pl.when(jnp.logical_not(own))
            def _():
                away.start()

            @pl.when(own)
            def _():
                local.start()

            out_waits.append((own, away))

    def store(n, sh, value, add=False):
        s_rows = slice(256 * sh, 256 * sh + 256)
        for block in range(2):
            new = value[:, 128 * block : 128 * block + 128]
            parts[n, block, s_rows, :] = parts[n, block, s_rows, :] + new if add else new

    def over_in(d, k):
        for way in (1, -1):
            if (d, k, way) in over_copies:
                over_copies[d, k, way].wait_recv()

    q_own = z // 2
    lean = 1 - 2 * (z % 2)
    order = [q_own, (q_own + 4 - lean) % 4, (q_own + 4 + lean) % 4, (q_own + 2) % 4]

    own_over.wait_recv()
    over_in(1, 0)
    over_in(1, 1)
    tok_a.finish()
    tok_b.finish()
    project(order[0], 0)
    project(order[0], 1)
    event(2, 1)
    for sh in range(2):
        store(0, sh, near(sh, 0) + near(sh, 1))
    hi_over = states_second()
    over_in(2, 0)
    over_in(2, 1)
    project(order[1], 0)
    project(order[1], 1)
    event(3, 0)
    for sh in range(2):
        store(1, sh, near(sh, 0) + near(sh, 1))
    states_finish()
    for n in range(2):
        enter(order[n])
        for sh in range(2):
            store(n, sh, far(sh), True)
            deliver(n, order[n], sh)
    over_in(3, 0)
    project(order[2], 0)
    event(3, 1)
    for sh in range(2):
        store(2, sh, near(sh, 0))
    over_in(3, 1)
    project(order[2], 1)
    event(4, 0)
    enter(order[2])
    for sh in (1, 0):
        store(2, sh, near(sh, 1) + far(sh), True)
        deliver(2, order[2], sh)
    over_in(4, 0)
    project(order[3], 0)
    event(4, 1)
    for sh in range(2):
        store(3, sh, near(sh, 0))
    over_in(4, 1)
    project(order[3], 1)
    enter(order[3])
    for sh in (1, 0):
        store(3, sh, near(sh, 1) + far(sh), True)
        deliver(3, order[3], sh)

    for n in range(4):
        q = order[n]

        @pl.when(q // 2 == c)
        def _():
            cols = pl.ds(pl.multiple_of((q % 2) * 128, 128), 128)
            for sh in (1, 0):
                s_rows = slice(256 * sh, 256 * sh + 256)
                for y_of in range(NY):
                    ref = arrived.at[y_of, s_rows, cols]
                    pltpu.make_async_copy(ref, ref, o_recv.at[y_of, 2 * (q % 2) + sh]).wait()
                total = arrived[0, s_rows, cols] + arrived[1, s_rows, cols]
                total = total + arrived[2, s_rows, cols] + arrived[3, s_rows, cols]
                out_ref[s_rows, cols] = total.astype(BF16)

    tok_a.drain()

    @pl.when(x // 2 != c)
    def _():
        hi_over.wait_send()

    for copy in unit_copies + total_copies + enter_copies + m_wait + ms_wait + g_wait + sent + [own_over]:
        copy.wait_send()
    for own, away in out_waits:

        @pl.when(jnp.logical_not(own))
        def _():
            away.wait_send()


def per_device(out_grad, filter_mats, coeffs, pole_rates):
    dma = pltpu.SemaphoreType.DMA
    vmem = pl.BlockSpec(memory_space=pltpu.VMEM)
    return pl.pallas_call(
        kernel,
        out_shape=jax.ShapeDtypeStruct((TOK, WIDE), BF16),
        in_specs=[vmem] * 4,
        out_specs=vmem,
        scratch_shapes=[
            pltpu.VMEM((NX, ROWS, D), BF16),
            pltpu.VMEM((4, 2, 2, 128, D), BF16),
            pltpu.VMEM((TOK, D), BF16),
            pltpu.VMEM((TOK, D), BF16),
            pltpu.VMEM((D, 256), BF16),
            pltpu.VMEM((D, 256), BF16),
            pltpu.VMEM((4, 2, TOK, 128), F32),
            pltpu.VMEM((NY, TOK, WIDE), F32),
            pltpu.VMEM((TOK, 128), BF16),
            pltpu.VMEM((TOK, 128), BF16),
            pltpu.VMEM((128, 256), BF16),
            pltpu.VMEM((128, 256), BF16),
            pltpu.VMEM((4, 128, 128), F32),
            pltpu.VMEM((8, 128), F32),
            pltpu.VMEM((16, 128), F32),
            pltpu.VMEM((128, 128), F32),
            pltpu.VMEM((UNITS, 8, 128), F32),
            pltpu.VMEM((UNITS, 8, 128), F32),
            pltpu.VMEM((NZ, 3, 8, 128), F32),
            pltpu.VMEM((3, 8, 128), F32),
            pltpu.VMEM((NX, 3, 8, 128), F32),
            pltpu.VMEM((NZ, 3, 8, 128), F32),
            pltpu.VMEM((UNITS, 8, 128), F32),
            dma((2, 4)), dma((2, 4)), dma((2, 8)), dma((2, 8)),
            dma((2, 8)), dma((2, 16)), dma((2, 3)), dma((2, 3)),
            dma((17,)), dma((18,)),
            dma((16,)), dma((16,)), dma((17,)), dma((17,)),
            dma((NZ,)), dma((NZ,)), dma((NX,)), dma((NX,)), dma((NZ,)), dma((NZ,)),
            dma((16,)), dma((NY, 4)), dma((1,)),
        ],
        compiler_params=pltpu.CompilerParams(
            collective_id=0, has_side_effects=True, vmem_limit_bytes=60 * 1024 * 1024
        ),
        name="spectral_grad",
    )(out_grad, filter_mats, pole_rates.reshape(1, POLES), coeffs)


def solution(mesh):
    placed = (P("ctx", "grp"), P("grp", "ctx", None), P(), P())
    return jax.shard_map(
        per_device, mesh=mesh, in_specs=placed, out_specs=P("ctx", "grp"), check_vma=False
    )
```

time: 492 us -> 82.2 us (0.17)
  waiting for transfers between devices: 262 us -> 0 us
  blocking collectives: 120 us -> 0 us
  Pallas kernels: 0 us -> 80.4 us
  matrix products: 43.8 us -> 0 us
  other arithmetic: 42.7 us -> 0 us
  between operations: 13.9 us -> 0.01 us
    all_gather x3 -> x0, waiting for transfers between devices: 198 us -> none  [the longest x1 142 us: per_device(): lax.all_gather(filter_mats, 'ctx', axis=1, tiled=True)]
    unnamed x1 -> x0, blocking collectives: 120 us -> none
    pallas_call x0 -> x1, Pallas kernels: none -> 80.4 us  [per_device(): pl.pallas_call(kernel, out_shape=jax.ShapeDtypeStruct((TOK, WIDE), BF16),...]
    psum x1 -> x0, waiting for transfers between devices: 62.5 us -> none  [per_device(): pole_sum = lax.psum(stacked[length:], 'grp')]
    dot_general x5 -> x0, matrix products: 43.8 us -> none  [the longest x1 17.5 us: per_device(): jnp.einsum('kts,kti->si', kernel_mat, proj_grad, precision=exact_prec)]
    select_n x32 -> x0, other arithmetic: 39.9 us -> none  [step(): return jax.tree.map(lambda a, b: jnp.where(reached, a, b), new, before)]
  transfers between devices with their start and end apart: 5 -> 0, of which waited for: 4 -> 0; matrix products, arithmetic and copies ran while one was open for 13% -> 0% of each run, Pallas kernels for 0% -> 0%
where the time goes in v2:
time: 82.2 us; the launch traced here: 82.1 us
  Pallas kernels  80.4 us (98%)
  local copies, waits for them, and re-layouts  1.67 us (2%)
    pallas_call x1, Pallas kernels, per_device(): pl.pallas_call(kernel, out_shape=jax.ShapeDtypeStruct((TOK, WIDE), BF16),...  80.4 us
    unnamed x1, local copies, waits for them, and re-layouts  1.67 us

profile of v2, /device:TPU:1, one launch (start us, length us, event | category | flops | bytes accessed | tf_op | source)
XLA Modules:
  0.0 82.1 jit_solution(10805976344272008367)
XLA Ops:
  0.0 80.4 %spectral_grad.1 = bf16[512,256]{1,0:T(8,128)(2,1)} custom-call(bf16[512,256]{1,0:T(8,128)(2,1)} %g_ref.1, bf16[2,64,2048]{2,1,0:T(8,128)(2,1)} %m_ref.1, f32[1,80]{1,0:T(1,128)} %bitcast.1, f32[16,80]{1,0:T(8,128)} %coeffs_ref.1), custom_call_target="tpu_custom_call" | custom-call | tf_op jit(solution)/shard_map/spectral_grad/pallas_call | solution.py:633
  80.4 1.7 %copy.6 = bf16[512,256]{1,0:T(8,128)(2,1)} copy(bf16[512,256]{1,0:T(8,128)(2,1)} %spectral_grad.1) | data formatting | bytes 524288

commit v3 on v2

--- a/solution.py
+++ b/solution.py
@@ -41,7 +41,7 @@
     total_out, total_in, enter_out, enter_in,
     p1_send, p1_recv, p2_send, p2_recv, rl_send, rl_recv, sh_send, sh_recv,
     g_send, g_recv, m_send, m_recv, ms_send, ms_recv, u_send, u_recv,
-    t_send, t_recv, e_send, e_recv, o_send, o_recv, l_sem,
+    t_send, t_recv, e_send, e_recv, o_send, o_recv, l_sem, near_sem,
 ):
     ctx, grp = lax.axis_index("ctx"), lax.axis_index("grp")
     x, z, y, c = ctx // NZ, ctx % NZ, grp // 2, grp % 2
@@ -63,32 +63,12 @@
     side = pl.ds(pl.multiple_of(c * HALF, HALF), HALF)
 
     barrier = pltpu.get_barrier_semaphore()
-    partners = [device(z_to=(z + d) % NZ) for d in range(1, NZ)]
-    partners += [device(x_to=(x + d) % NX) for d in range(1, NX)]
-    partners += [device(y_to=(y + d) % NY) for d in range(1, NY)]
+    partners = [device(z_to=(z + d) % NZ) for d in (1, NZ - 1)]
+    partners += [device(x_to=(x + d) % NX) for d in (1, NX - 1)]
+    partners += [device(y_to=(y + d) % NY) for d in (1, NY - 1)]
     partners += [sibling]
     for target in partners:
         pl.semaphore_signal(barrier, inc=1, device_id=target, device_id_type=MESH)
-    for block in range(2):
-        for half in range(2):
-            own = jnp.logical_and(jnp.logical_and(2 * c + block == x, x == y), half == c)
-
-            @pl.when(jnp.logical_not(own))
-            def _():
-                pl.semaphore_signal(
-                    barrier, inc=1, device_id_type=MESH,
-                    device_id=device(x_to=2 * c + block, y_to=x, c_to=half),
-                )
-    for y_of in range(NY):
-        own = jnp.logical_and(jnp.logical_and(y == x, y_of == y), x // 2 == c)
-
-        @pl.when(jnp.logical_not(own))
-        def _():
-            pl.semaphore_signal(
-                barrier, inc=1, device_id_type=MESH,
-                device_id=device(x_to=y, y_to=y_of, c_to=x // 2),
-            )
-    self_out = jnp.logical_and(x == y, x // 2 == c)
 
     low = pl.ds(pl.multiple_of(64 * (z % 2), 64), 64)
     for c_of in range(2):
@@ -117,8 +97,51 @@
             unit_out[group * 2 + half] = state[8 * group : 8 * group + 8, 128 * half : 128 * half + 128]
             unit_rates[group * 2 + half] = rates_col[8 * group : 8 * group + 8, :]
 
-    pl.semaphore_wait(barrier, jnp.where(self_out, len(partners) + 6, len(partners) + 8))
-
+    pl.semaphore_wait(barrier, len(partners))
+
+    def piece(z_of, d, k, way):
+        start, size = 64 * (z_of % 2), 64
+        if d == 4:
+            start, size = start + 16 * (1 - way), 32
+        return mats.at[z_of // 2, k, c, pl.ds(pl.multiple_of(start, 32), size), :]
+
+    m_wait, ms_wait = [], []
+
+    def ring(d, k, way):
+        z_of = (z + NZ - way * (d - 1)) % NZ
+        ref = piece(z_of, d, k, way)
+        i = ((d - 1) * 2 + k) * 2 + (way + 1) // 2
+        copy = remote(ref, ref, m_send.at[i], m_recv.at[i], device(z_to=(z + NZ + way) % NZ))
+        copy.start()
+        m_wait.append(copy)
+        return copy
+
+    def arrive(copy, d, k, way):
+        z_of = (z + NZ - way * d) % NZ
+        ref = piece(z_of, d, k, way)
+        i = ((d - 1) * 2 + k) * 2 + (way + 1) // 2
+        copy.wait_recv()
+        over = remote(ref, ref, ms_send.at[i], ms_recv.at[i], sibling)
+        over.start()
+        ms_wait.append(over)
+        return over
+
+    ring_copies, over_copies = {}, {}
+
+    def event(d, k):
+        for way in (1, -1):
+            over_copies[d, k, way] = arrive(ring_copies[d, k, way], d, k, way)
+            if d < 4:
+                ring_copies[d + 1, k, way] = ring(d + 1, k, way)
+
+    for way in (1, -1):
+        ring_copies[1, 0, way] = ring(1, 0, way)
+    for step in range(3):
+        for d in (1, NZ - 1):
+            pl.semaphore_signal(
+                near_sem.at[step], inc=1, device_id=device(z_to=(z + d) % NZ), device_id_type=MESH
+            )
+        pl.semaphore_wait(near_sem.at[step], 2)
     unit_copies = []
     for d in range(1, NZ):
         to = (z + d) % NZ
@@ -213,19 +236,21 @@
                 )
 
         def start(self):
-            ref = self.ref(0, 0, self.rows)
-            self.p1[0] = self.copy(self.src, ref, 0, self.hop1(1))
-            self.p1[1] = self.copy(self.src, ref, 1, self.hop1(-1))
+            halves = ((self.first, self.src.at[0:128, :]), (self.last, self.src.at[128:256, :]))
+            for i in range(2):
+                for at, way in ((0, 1), (1, -1)):
+                    rows, src = halves[i ^ at]
+                    self.p1[at, i] = self.copy(src, self.ref(0, 0, rows), 2 * i + at, self.hop1(way))
 
         def mid(self):
             for i, way, rows in ((0, 1, self.first), (1, -1, self.last)):
-                self.p1[i].wait_recv()
+                self.p1[i, 0].wait_recv()
                 ref = self.ref(-way, 0, rows)
-                self.p1[i + 2] = self.copy(ref, ref, i + 2, self.hop1(way))
+                self.p1[i, 2] = self.copy(ref, ref, i + 4, self.hop1(way))
 
         def opposite(self):
-            self.p1[2].wait_recv()
-            self.p1[3].wait_recv()
+            self.p1[0, 2].wait_recv()
+            self.p1[1, 2].wait_recv()
             self.onward(3)
 
         def relay(self, j):
@@ -306,51 +331,14 @@
 
     tok_a.start()
     tok_b.start()
+
     tok_a.onward(0, tok_a.src)
     tok_b.onward(0, tok_b.src)
-
-    def piece(z_of, d, k, way):
-        start, size = 64 * (z_of % 2), 64
-        if d == 4:
-            start, size = start + 16 * (1 - way), 32
-        return mats.at[z_of // 2, k, c, pl.ds(pl.multiple_of(start, 32), size), :]
-
-    m_wait, ms_wait = [], []
-
-    def ring(d, k, way):
-        z_of = (z + NZ - way * (d - 1)) % NZ
-        ref = piece(z_of, d, k, way)
-        i = ((d - 1) * 2 + k) * 2 + (way + 1) // 2
-        copy = remote(ref, ref, m_send.at[i], m_recv.at[i], device(z_to=(z + NZ + way) % NZ))
-        copy.start()
-        m_wait.append(copy)
-        return copy
-
-    def arrive(copy, d, k, way):
-        z_of = (z + NZ - way * d) % NZ
-        ref = piece(z_of, d, k, way)
-        i = ((d - 1) * 2 + k) * 2 + (way + 1) // 2
-        copy.wait_recv()
-        over = remote(ref, ref, ms_send.at[i], ms_recv.at[i], sibling)
-        over.start()
-        ms_wait.append(over)
-        return over
-
-    ring_copies = {}
-    for k in range(2):
-        for way in (1, -1):
-            ring_copies[1, k, way] = ring(1, k, way)
+    for way in (1, -1):
+        ring_copies[1, 1, way] = ring(1, 1, way)
     own_ref = mats.at[z // 2, :, c, low, :]
     own_over = remote(own_ref, own_ref, ms_send.at[16], ms_recv.at[16], sibling)
     own_over.start()
-
-    over_copies = {}
-
-    def event(d, k):
-        for way in (1, -1):
-            over_copies[d, k, way] = arrive(ring_copies[d, k, way], d, k, way)
-            if d < 4:
-                ring_copies[d + 1, k, way] = ring(d + 1, k, way)
 
     own_units = pl.ds(3 * z, 3)
     total_copies, enter_copies = [], []
@@ -435,7 +423,9 @@
     tok_b.mid()
     hand_on()
     for j in (1, 2):
+        tok_a.p1[j - 1, 1].wait_recv()
         tok_a.onward(j)
+        tok_b.p1[j - 1, 1].wait_recv()
         tok_b.onward(j)
     for k in range(4):
         taps(0, k)
@@ -455,18 +445,18 @@
     state_hi[...] = jnp.zeros_like(state_hi)
     state_lo[...] = jnp.zeros_like(state_lo)
     store_enter()
-    states_first()
     tok_a.relay(3)
     tok_b.relay(3)
+    states_first()
     tok_a.share()
     tok_b.share()
     more_taps((2,))
     event(2, 0)
     more_taps((3,))
 
-    def project(q, kk):
+    def project(q, kk, ths=(0, 1)):
         weights = mats[q, kk].reshape(256, D)
-        parts_of = [(block, th) for block in range(2) for th in range(2)]
+        parts_of = [(block, th) for block in range(2) for th in ths]
         tiles = [mm(grads[block, 256 * th : 256 * th + 256, :], weights, NT) for block, th in parts_of]
         for (block, th), tile in zip(parts_of, tiles):
             high, rest = split(tile)
@@ -554,46 +544,47 @@
     over_in(1, 1)
     tok_a.finish()
     tok_b.finish()
+    hi_over = states_second()
     project(order[0], 0)
     project(order[0], 1)
     event(2, 1)
     for sh in range(2):
         store(0, sh, near(sh, 0) + near(sh, 1))
-    hi_over = states_second()
     over_in(2, 0)
     over_in(2, 1)
     project(order[1], 0)
+    event(3, 0)
     project(order[1], 1)
-    event(3, 0)
+    states_finish()
+    enter(order[0])
     for sh in range(2):
-        store(1, sh, near(sh, 0) + near(sh, 1))
-    states_finish()
-    for n in range(2):
-        enter(order[n])
-        for sh in range(2):
-            store(n, sh, far(sh), True)
-            deliver(n, order[n], sh)
+        store(0, sh, far(sh), True)
+        deliver(0, order[0], sh)
+    enter(order[1])
+    for sh in (1, 0):
+        store(1, sh, near(sh, 0) + near(sh, 1) + far(sh))
+        deliver(1, order[1], sh)
+    event(3, 1)
     over_in(3, 0)
     project(order[2], 0)
-    event(3, 1)
     for sh in range(2):
         store(2, sh, near(sh, 0))
+    event(4, 0)
     over_in(3, 1)
     project(order[2], 1)
-    event(4, 0)
     enter(order[2])
     for sh in (1, 0):
         store(2, sh, near(sh, 1) + far(sh), True)
         deliver(2, order[2], sh)
+    event(4, 1)
     over_in(4, 0)
     project(order[3], 0)
-    event(4, 1)
     for sh in range(2):
         store(3, sh, near(sh, 0))
     over_in(4, 1)
-    project(order[3], 1)
     enter(order[3])
     for sh in (1, 0):
+        project(order[3], 1, (sh,))
         store(3, sh, near(sh, 1) + far(sh), True)
         deliver(3, order[3], sh)
 
@@ -659,12 +650,12 @@
             pltpu.VMEM((NX, 3, 8, 128), F32),
             pltpu.VMEM((NZ, 3, 8, 128), F32),
             pltpu.VMEM((UNITS, 8, 128), F32),
-            dma((2, 4)), dma((2, 4)), dma((2, 8)), dma((2, 8)),
+            dma((2, 6)), dma((2, 6)), dma((2, 8)), dma((2, 8)),
             dma((2, 8)), dma((2, 16)), dma((2, 3)), dma((2, 3)),
             dma((17,)), dma((18,)),
             dma((16,)), dma((16,)), dma((17,)), dma((17,)),
             dma((NZ,)), dma((NZ,)), dma((NX,)), dma((NX,)), dma((NZ,)), dma((NZ,)),
-            dma((16,)), dma((NY, 4)), dma((1,)),
+            dma((16,)), dma((NY, 4)), dma((1,)), pltpu.SemaphoreType.REGULAR((3,)),
         ],
         compiler_params=pltpu.CompilerParams(
             collective_id=0, has_side_effects=True, vmem_limit_bytes=60 * 1024 * 1024

time: 82.2 us -> 80.2 us (0.976)
  Pallas kernels: 80.4 us -> 78.4 us
    pallas_call x1, Pallas kernels: 80.4 us -> 78.4 us  [per_device(): pl.pallas_call(kernel, out_shape=jax.ShapeDtypeStruct((TOK, WIDE), BF16),...]
where the time goes in v3:
time: 80.2 us; the launch traced here: 80.1 us
  Pallas kernels  78.4 us (98%)
  local copies, waits for them, and re-layouts  1.67 us (2%)
    pallas_call x1, Pallas kernels, per_device(): pl.pallas_call(kernel, out_shape=jax.ShapeDtypeStruct((TOK, WIDE), BF16),...  78.4 us
    unnamed x1, local copies, waits for them, and re-layouts  1.67 us

profile of v3, /device:TPU:1, one launch (start us, length us, event | category | flops | bytes accessed | tf_op | source)
XLA Modules:
  0.0 80.1 jit_solution(15259615062408890260)
XLA Ops:
  0.0 78.4 %spectral_grad.1 = bf16[512,256]{1,0:T(8,128)(2,1)} custom-call(bf16[512,256]{1,0:T(8,128)(2,1)} %g_ref.1, bf16[2,64,2048]{2,1,0:T(8,128)(2,1)} %m_ref.1, f32[1,80]{1,0:T(1,128)} %bitcast.1, f32[16,80]{1,0:T(8,128)} %coeffs_ref.1), custom_call_target="tpu_custom_call" | custom-call | tf_op jit(solution)/shard_map/spectral_grad/pallas_call | solution.py:624
  78.4 1.7 %copy.6 = bf16[512,256]{1,0:T(8,128)(2,1)} copy(bf16[512,256]{1,0:T(8,128)(2,1)} %spectral_grad.1) | data formatting | bytes 524288

commit v4 on v3

--- a/solution.py
+++ b/solution.py
@@ -35,13 +35,13 @@
 
 
 def kernel(
-    g_ref, m_ref, rates_ref, coeffs_ref, out_ref,
-    grads, mats, kern_hi, kern_lo, proj_hi, proj_lo, parts, arrived, edge_hi, edge_lo,
+    g_hbm, m_hbm, rates_hbm, coeffs_hbm, out_ref,
+    g_ref, rates_ref, coeffs_ref, grads, mats, kern_hi, kern_lo, proj_hi, proj_lo, parts, arrived, edge_hi, edge_lo,
     state_hi, state_lo, coef_col, rates_row, coef_row, rates_col, unit_rates, unit_out, unit_in,
     total_out, total_in, enter_out, enter_in,
     p1_send, p1_recv, p2_send, p2_recv, rl_send, rl_recv, sh_send, sh_recv,
     g_send, g_recv, m_send, m_recv, ms_send, ms_recv, u_send, u_recv,
-    t_send, t_recv, e_send, e_recv, o_send, o_recv, l_sem, near_sem,
+    t_send, t_recv, e_send, e_recv, o_send, o_recv, l_sem, i_sem, near_sem,
 ):
     ctx, grp = lax.axis_index("ctx"), lax.axis_index("grp")
     x, z, y, c = ctx // NZ, ctx % NZ, grp // 2, grp % 2
@@ -71,11 +71,25 @@
         pl.semaphore_signal(barrier, inc=1, device_id=target, device_id_type=MESH)
 
     low = pl.ds(pl.multiple_of(64 * (z % 2), 64), 64)
+    fetches = [
+        pltpu.make_async_copy(rates_hbm, rates_ref, i_sem.at[0]),
+        pltpu.make_async_copy(coeffs_hbm, coeffs_ref, i_sem.at[1]),
+        pltpu.make_async_copy(g_hbm, g_ref, i_sem.at[2]),
+    ]
     for c_of in range(2):
         for y_of in range(NY):
-            mats[z // 2, :, c, low, (c_of * NY + y_of) * WIDE : (c_of * NY + y_of + 1) * WIDE] = m_ref[
-                :, :, (y_of * 2 + c_of) * WIDE : (y_of * 2 + c_of + 1) * WIDE
-            ]
+            to, at = (c_of * NY + y_of) * WIDE, (y_of * 2 + c_of) * WIDE
+            fetches.append(
+                pltpu.make_async_copy(
+                    m_hbm.at[:, :, at : at + WIDE],
+                    mats.at[z // 2, :, c, low, to : to + WIDE],
+                    i_sem.at[3 + c_of * NY + y_of],
+                )
+            )
+    for fetch in fetches:
+        fetch.start()
+    for fetch in fetches[0:3]:
+        fetch.wait()
     own_copy = pltpu.make_async_copy(g_ref, grads.at[slot(x), 0:TOK, col(y)], l_sem.at[0])
     own_copy.start()
 
@@ -97,6 +111,8 @@
             unit_out[group * 2 + half] = state[8 * group : 8 * group + 8, 128 * half : 128 * half + 128]
             unit_rates[group * 2 + half] = rates_col[8 * group : 8 * group + 8, :]
 
+    for fetch in fetches[3:]:
+        fetch.wait()
     pl.semaphore_wait(barrier, len(partners))
 
     def piece(z_of, d, k, way):
@@ -619,14 +635,18 @@
 
 
 def per_device(out_grad, filter_mats, coeffs, pole_rates):
+    held = (out_grad, filter_mats, pole_rates.reshape(1, POLES), coeffs)
     dma = pltpu.SemaphoreType.DMA
     vmem = pl.BlockSpec(memory_space=pltpu.VMEM)
     return pl.pallas_call(
         kernel,
         out_shape=jax.ShapeDtypeStruct((TOK, WIDE), BF16),
-        in_specs=[vmem] * 4,
+        in_specs=[pl.BlockSpec(memory_space=pltpu.MemorySpace.HBM)] * 4,
         out_specs=vmem,
         scratch_shapes=[
+            pltpu.VMEM((TOK, WIDE), BF16),
+            pltpu.VMEM((1, POLES), F32),
+            pltpu.VMEM((16, POLES), F32),
             pltpu.VMEM((NX, ROWS, D), BF16),
             pltpu.VMEM((4, 2, 2, 128, D), BF16),
             pltpu.VMEM((TOK, D), BF16),
@@ -655,13 +675,13 @@
             dma((17,)), dma((18,)),
             dma((16,)), dma((16,)), dma((17,)), dma((17,)),
             dma((NZ,)), dma((NZ,)), dma((NX,)), dma((NX,)), dma((NZ,)), dma((NZ,)),
-            dma((16,)), dma((NY, 4)), dma((1,)), pltpu.SemaphoreType.REGULAR((3,)),
+            dma((16,)), dma((NY, 4)), dma((1,)), dma((11,)), pltpu.SemaphoreType.REGULAR((3,)),
         ],
         compiler_params=pltpu.CompilerParams(
-            collective_id=0, has_side_effects=True, vmem_limit_bytes=60 * 1024 * 1024
+            collective_id=0, has_side_effects=True, vmem_limit_bytes=44 * 1024 * 1024
         ),
         name="spectral_grad",
-    )(out_grad, filter_mats, pole_rates.reshape(1, POLES), coeffs)
+    )(*[pltpu.with_memory_space_constraint(v, pltpu.MemorySpace.HBM) for v in held])
 
 
 def solution(mesh):

time: 80.2 us -> 77.6 us (0.968)
  Pallas kernels: 78.4 us -> 76.7 us
  local copies, waits for them, and re-layouts: 1.67 us -> 0.71 us
    pallas_call x1, Pallas kernels: 78.4 us -> 76.7 us  [per_device(): pl.pallas_call(kernel, out_shape=jax.ShapeDtypeStruct((TOK, WIDE), BF16),...]
    unnamed x1, local copies, waits for them, and re-layouts: 1.67 us -> 0.71 us
where the time goes in v4:
time: 77.6 us; the launch traced here: 77.4 us
  Pallas kernels  76.7 us (99%)
    pallas_call x1, Pallas kernels, per_device(): pl.pallas_call(kernel, out_shape=jax.ShapeDtypeStruct((TOK, WIDE), BF16),...  76.7 us

profile of v4, /device:TPU:1, one launch (start us, length us, event | category | flops | bytes accessed | tf_op | source)
XLA Modules:
  0.0 77.4 jit_solution(10062143125273812306)
XLA Ops:
  0.0 76.7 %spectral_grad.1 = bf16[512,256]{1,0:T(8,128)(2,1)S(1)} custom-call(bf16[512,256]{1,0:T(8,128)(2,1)} %g_hbm.1, bf16[2,64,2048]{2,1,0:T(8,128)(2,1)} %m_hbm.1, f32[1,80]{1,0:T(1,128)} %bitcast.1, f32[16,80]{1,0:T(8,128)} %coeffs_hbm.1), custom_call_target="tpu_custom_call" | custom-call | tf_op jit(solution)/shard_map/spectral_grad/pallas_call | solution.py:641
  76.7 0.7 copy.6

commit v5 on v4

--- a/solution.py
+++ b/solution.py
@@ -558,9 +558,9 @@
     own_over.wait_recv()
     over_in(1, 0)
     over_in(1, 1)
+    hi_over = states_second()
     tok_a.finish()
     tok_b.finish()
-    hi_over = states_second()
     project(order[0], 0)
     project(order[0], 1)
     event(2, 1)

time: 77.6 us -> 77.1 us (level)
  no operation moved by 1% of the time
where the time goes in v5:
time: 77.1 us; the launch traced here: 77 us
  Pallas kernels  76.3 us (99%)
    pallas_call x1, Pallas kernels, per_device(): pl.pallas_call(kernel, out_shape=jax.ShapeDtypeStruct((TOK, WIDE), BF16),...  76.3 us

profile of v5, /device:TPU:1, one launch (start us, length us, event | category | flops | bytes accessed | tf_op | source)
XLA Modules:
  0.0 77.0 jit_solution(7712079494205553227)
XLA Ops:
  0.0 76.3 %spectral_grad.1 = bf16[512,256]{1,0:T(8,128)(2,1)S(1)} custom-call(bf16[512,256]{1,0:T(8,128)(2,1)} %g_hbm.1, bf16[2,64,2048]{2,1,0:T(8,128)(2,1)} %m_hbm.1, f32[1,80]{1,0:T(1,128)} %bitcast.1, f32[16,80]{1,0:T(8,128)} %coeffs_hbm.1), custom_call_target="tpu_custom_call" | custom-call | tf_op jit(solution)/shard_map/spectral_grad/pallas_call | solution.py:641
  76.3 0.7 copy.6
